TPU v7x, 512 devices: a whole 4x4x16 slice. The times are simulated.
512 devices in a mesh: bulk: 32 (over z, core), blk: 16 (over y, x).
Axes of the slice: x: 4, y: 4, z: 16, core: 2. Of those that a mesh axis runs over, the one named last changes fastest.
Arguments:
- factor: float32 [131072, 4096], P(('bulk', 'blk')), parts along dimension 0, as said below
- initial: float32 [131072, 128], P(('bulk', 'blk')), parts along dimension 0, may hold values from -6 to 6
- bounds: float32 [64], P('bulk'), parts along dimension 0, may hold values from 0 to 15.5, as said below
Outputs:
- basis_rows: float32 [131072, 128], P(('bulk', 'blk')), parts along dimension 0
- projected: float32 [4096, 128], P('bulk'), parts along dimension 0
- residual: float32 [131072, 128], P(('bulk', 'blk')), parts along dimension 0
There are 32 independent parts, one for each index of `bulk`. A program takes and returns all parts, laid end to end along the dimension named above; each array names one. Nothing has to cross between parts.
Inputs may be any that keep to these rules, and one draw needn't show every extreme that they name: factor is symmetric. `bounds`: the upper end exceeds the lower end by 14 or more.
All inputs are finite; a program needn't handle non-finite values.
Results may differ from a plain program's by a relative error of at most 0.0003.
Values sent between devices are 32-bit elements; how exact they have to be, the bound alone decides.
A program may use at most 64 MiB of HBM per device.

v0:
```python
import jax
import jax.numpy as jnp
from jax import lax
from jax.sharding import PartitionSpec as P

DEGREE = 8


def local_dot(left_side, right_side):
    return jnp.dot(
        left_side, right_side, precision=lax.Precision.HIGHEST, preferred_element_type=jnp.float32
    )


def lower_solve(cholesky_low, right_side):
    return lax.linalg.triangular_solve(cholesky_low, right_side, left_side=True, lower=True)


def apply_factor(factor_rows, vectors):
    return local_dot(factor_rows, lax.all_gather(vectors, "blk", axis=0, tiled=True))


def local(factor, initial, bounds):
    centre = (bounds[0] + bounds[1]) / 2.0
    radius = (bounds[1] - bounds[0]) / 2.0
    previous = initial
    current = (apply_factor(factor, initial) - centre * initial) / radius
    for order_step in range(DEGREE - 1):
        scaled = (apply_factor(factor, current) - centre * current) / radius
        following = 2.0 * scaled - previous
        previous = current
        current = following
    gram_matrix = lax.psum(
        lax.dot_general(
            current,
            current,
            (((0,), (0,)), ((), ())),
            precision=lax.Precision.HIGHEST,
            preferred_element_type=jnp.float32,
        ),
        "blk",
    )
    cholesky_low = jnp.linalg.cholesky(gram_matrix)
    basis_rows = lower_solve(cholesky_low, current.T).T
    mapped = apply_factor(factor, basis_rows)
    projected = lax.psum(
        lax.dot_general(
            basis_rows,
            mapped,
            (((0,), (0,)), ((), ())),
            precision=lax.Precision.HIGHEST,
            preferred_element_type=jnp.float32,
        ),
        "blk",
    )
    residual = mapped - local_dot(basis_rows, projected)
    return (basis_rows, projected, residual)


def solution(mesh):
    in_specs = (P(("bulk", "blk"), None), P(("bulk", "blk"), None), P("bulk"))
    out_specs = (P(("bulk", "blk"), None), P("bulk", None), P(("bulk", "blk"), None))
    return jax.shard_map(local, mesh=mesh, in_specs=in_specs, out_specs=out_specs, check_vma=False)
```

profile of v0, /device:TPU:2, one launch (start us, length us, event | category | flops | bytes accessed | tf_op | source)
XLA Modules:
  0.0 879.8 jit_solution(10453286735526572936)
XLA Ops:
  7.2 0.0 all-gather.10.cloned.1.call-start
  7.2 0.7 all-gather.10.cloned.1.call-update
  7.9 0.0 all-gather.12.cloned.1.call-start
  7.9 1.3 fusion.33
  11.9 63.6 %all-gather.10.cloned.1.call-done = f32[4096,128]{1,0:T(8,128)} async-done(((f32[256,128]{1,0:T(8,128)}), f32[4096,128]{1,0:T(8,128)}) %all-gather.10.cloned.1.call-update) | async-done | bytes 2097168 | tf_op jit(solution)/shard_map/all_gather | solution.py:20
  75.4 7.0 fusion.28
  82.4 0.0 all-gather.12.cloned.1.call-update
  82.4 0.0 copy-start.6
  82.4 0.0 all-gather.14.cloned.1.call-start
  82.5 59.8 %all-gather.12.cloned.1.call-done = f32[4096,128]{1,0:T(8,128)} async-done(((f32[256,128]{1,0:T(8,128)}), f32[4096,128]{1,0:T(8,128)}) %all-gather.12.cloned.1.call-update) | async-done | bytes 2097168 | tf_op jit(solution)/shard_map/all_gather | solution.py:20
  142.3 7.0 fusion.27
  149.2 0.0 all-gather.14.cloned.1.call-update
  149.3 0.0 copy-start.5
  149.3 0.0 all-gather.16.cloned.1.call-start
  149.3 59.8 %all-gather.14.cloned.1.call-done = f32[4096,128]{1,0:T(8,128)} async-done(((f32[256,128]{1,0:T(8,128)}), f32[4096,128]{1,0:T(8,128)}) %all-gather.14.cloned.1.call-update) | async-done | bytes 2097168 | tf_op jit(solution)/shard_map/all_gather | solution.py:20
  209.1 0.0 copy-done.6
  209.1 7.0 fusion.23
  216.1 0.0 all-gather.16.cloned.1.call-update
  216.1 0.0 copy-start.2
  216.1 0.5 all-gather.18.cloned.1.call-start
  216.6 59.3 %all-gather.16.cloned.1.call-done = f32[4096,128]{1,0:T(8,128)} async-done(((f32[256,128]{1,0:T(8,128)}), f32[4096,128]{1,0:T(8,128)}) %all-gather.16.cloned.1.call-update) | async-done | bytes 2097168 | tf_op jit(solution)/shard_map/all_gather | solution.py:20
  276.0 7.0 fusion.19
  282.9 0.0 all-gather.18.cloned.1.call-update
  283.0 0.0 copy-start.3
  283.0 0.0 all-gather.20.cloned.1.call-start
  283.0 59.8 %all-gather.18.cloned.1.call-done = f32[4096,128]{1,0:T(8,128)} async-done(((f32[256,128]{1,0:T(8,128)}), f32[4096,128]{1,0:T(8,128)}) %all-gather.18.cloned.1.call-update) | async-done | bytes 2097168 | tf_op jit(solution)/shard_map/all_gather | solution.py:20
  342.8 7.0 fusion.15
  349.8 0.0 all-gather.20.cloned.1.call-update
  349.8 0.0 copy-start.4
  349.8 0.0 all-gather.22.cloned.1.call-start
  349.9 59.8 %all-gather.20.cloned.1.call-done = f32[4096,128]{1,0:T(8,128)} async-done(((f32[256,128]{1,0:T(8,128)}), f32[4096,128]{1,0:T(8,128)}) %all-gather.20.cloned.1.call-update) | async-done | bytes 2097168 | tf_op jit(solution)/shard_map/all_gather | solution.py:20
  409.7 7.0 fusion.11
  416.6 0.0 all-gather.22.cloned.1.call-update
  416.7 0.0 copy-start.1
  416.7 0.2 all-gather.24.cloned.1.call-start
  416.9 59.6 %all-gather.22.cloned.1.call-done = f32[4096,128]{1,0:T(8,128)} async-done(((f32[256,128]{1,0:T(8,128)}), f32[4096,128]{1,0:T(8,128)}) %all-gather.22.cloned.1.call-update) | async-done | bytes 2097168 | tf_op jit(solution)/shard_map/all_gather | solution.py:20
  476.5 7.0 fusion.7
  483.5 0.0 all-gather.24.cloned.1.call-update
  483.5 0.0 all-reduce.3.cloned.1.call-start
  483.6 59.8 %all-gather.24.cloned.1.call-done = f32[4096,128]{1,0:T(8,128)} async-done(((f32[256,128]{1,0:T(8,128)}), f32[4096,128]{1,0:T(8,128)}) %all-gather.24.cloned.1.call-update) | async-done | bytes 2097168 | tf_op jit(solution)/shard_map/all_gather | solution.py:20
  543.4 6.3 fusion.3
  549.7 1.0 fusion.34
  550.7 0.0 all-reduce.3.cloned.1.call-update
  550.7 0.3 all-gather.26.cloned.1.call-start
  551.0 111.0 %all-reduce.3.cloned.1.call-done = f32[128,128]{0,1:T(8,128)} async-done(((f32[128,128]{0,1:T(8,128)}), f32[128,128]{0,1:T(8,128)}) %all-reduce.3.cloned.1.call-update) | async-done | bytes 65552 | tf_op jit(solution)/shard_map/psum | solution.py:33
  662.0 0.9 copy.14
  662.9 0.9 fusion.32
  663.8 11.7 %cholesky.16 = f32[128,128]{1,0:T(8,128)S(1)} custom-call(f32[128,128]{1,0:T(8,128)S(1)} %fusion.32), custom_call_target="Cholesky" | custom-call | tf_op jit(solution)/shard_map/jit(cholesky)/cholesky | solution.py:43
  675.5 0.6 compare_reduce_fusion
  676.2 0.7 fusion.29
  676.8 9.8 %custom-call.6 = f32[1,128,128]{1,2,0:T(8,128)S(1)} custom-call(f32[1,128,128]{2,1,0:T(8,128)S(1)} %fusion.29), custom_call_target="InvertDiagBlocksLowerTriangular" | custom-call | tf_op jit(solution)/shard_map/triangular_solve | solution.py:16
  686.7 1.0 fusion.30
  687.6 0.0 all-gather.26.cloned.1.call-update
  687.7 0.0 copy-start
  687.7 0.0 all-reduce.5.cloned.1.call-start
  687.7 62.6 %all-gather.26.cloned.1.call-done = f32[4096,128]{0,1:T(8,128)} async-done(((f32[256,128]{0,1:T(8,128)}), f32[4096,128]{0,1:T(8,128)}) %all-gather.26.cloned.1.call-update) | async-done | bytes 2097168 | tf_op jit(solution)/shard_map/all_gather | solution.py:20
  750.3 7.1 fusion.35
  757.4 0.9 fusion.36
  758.3 0.0 all-reduce.5.cloned.1.call-update
  758.3 0.8 copy.16
  759.1 110.6 %all-reduce.5.cloned.1.call-done = f32[128,128]{1,0:T(8,128)} async-done(((f32[128,128]{1,0:T(8,128)}), f32[128,128]{1,0:T(8,128)}) %all-reduce.5.cloned.1.call-update) | async-done | bytes 65552 | tf_op jit(solution)/shard_map/psum | solution.py:46
  869.7 1.2 convolution_subtract_fusion.1
  870.9 0.8 copy.17
  871.6 1.5 copy.29
  (9 shorter events, 0.1 us)
Async XLA Ops:
  7.2 68.3 %all-gather.10.cloned.1.call-start = ((), (), s32[]{:S(2)}) async-start(), calls=%async_computation | async-start | bytes 2228224 | tf_op jit(solution)/shard_map/all_gather | solution.py:20
  7.9 134.4 %all-gather.12.cloned.1.call-start = ((), (), s32[]{:S(2)}) async-start(), calls=%async_computation.1 | async-start | bytes 2228224 | tf_op jit(solution)/shard_map/all_gather | solution.py:20
  75.4 66.9 %copy-start.7 = (f32[256,128]{1,0:T(8,128)S(1)}, f32[256,128]{1,0:T(8,128)}, u32[]{:S(2)}) copy-start(f32[256,128]{1,0:T(8,128)} %param.4) | copy-start | bytes 393220
  82.4 126.7 %copy-start.6 = (f32[256,128]{1,0:T(8,128)S(1)}, f32[256,128]{1,0:T(8,128)}, u32[]{:S(2)}) copy-start(f32[256,128]{1,0:T(8,128)} %fusion.28) | copy-start | bytes 393220
  82.4 126.7 %all-gather.14.cloned.1.call-start = ((), (), s32[]{:S(2)}) async-start(), calls=%async_computation.2 | async-start | bytes 2228224 | tf_op jit(solution)/shard_map/all_gather | solution.py:20
  149.3 126.7 %copy-start.5 = (f32[256,128]{1,0:T(8,128)S(1)}, f32[256,128]{1,0:T(8,128)}, u32[]{:S(2)}) copy-start(f32[256,128]{1,0:T(8,128)} %fusion.27) | copy-start | bytes 393220
  149.3 126.7 %all-gather.16.cloned.1.call-start = ((), (), s32[]{:S(2)}) async-start(), calls=%async_computation.3 | async-start | bytes 2228224 | tf_op jit(solution)/shard_map/all_gather | solution.py:20
  216.1 126.7 %copy-start.2 = (f32[256,128]{1,0:T(8,128)S(1)}, f32[256,128]{1,0:T(8,128)}, u32[]{:S(2)}) copy-start(f32[256,128]{1,0:T(8,128)} %fusion.23) | copy-start | bytes 393220
  216.1 126.7 %all-gather.18.cloned.1.call-start = ((), (), s32[]{:S(2)}) async-start(), calls=%async_computation.4 | async-start | bytes 2228224 | tf_op jit(solution)/shard_map/all_gather | solution.py:20
  283.0 126.7 %copy-start.3 = (f32[256,128]{1,0:T(8,128)S(1)}, f32[256,128]{1,0:T(8,128)}, u32[]{:S(2)}) copy-start(f32[256,128]{1,0:T(8,128)} %fusion.19) | copy-start | bytes 393220
  283.0 126.7 %all-gather.20.cloned.1.call-start = ((), (), s32[]{:S(2)}) async-start(), calls=%async_computation.5 | async-start | bytes 2228224 | tf_op jit(solution)/shard_map/all_gather | solution.py:20
  349.8 126.7 %copy-start.4 = (f32[256,128]{1,0:T(8,128)S(1)}, f32[256,128]{1,0:T(8,128)}, u32[]{:S(2)}) copy-start(f32[256,128]{1,0:T(8,128)} %fusion.15) | copy-start | bytes 393220
  349.8 126.7 %all-gather.22.cloned.1.call-start = ((), (), s32[]{:S(2)}) async-start(), calls=%async_computation.6 | async-start | bytes 2228224 | tf_op jit(solution)/shard_map/all_gather | solution.py:20
  416.7 126.7 %copy-start.1 = (f32[256,128]{1,0:T(8,128)S(1)}, f32[256,128]{1,0:T(8,128)}, u32[]{:S(2)}) copy-start(f32[256,128]{1,0:T(8,128)} %fusion.11) | copy-start | bytes 393220
  416.7 126.7 %all-gather.24.cloned.1.call-start = ((), (), s32[]{:S(2)}) async-start(), calls=%async_computation.7 | async-start | bytes 2228224 | tf_op jit(solution)/shard_map/all_gather | solution.py:20
  483.5 178.5 %all-reduce.3.cloned.1.call-start = ((), (), s32[]{:S(2)}) async-start(), calls=%async_computation.8 | async-start | bytes 131072 | tf_op jit(solution)/shard_map/psum | solution.py:33
  550.7 199.6 %all-gather.26.cloned.1.call-start = ((), (), s32[]{:S(2)}) async-start(), calls=%async_computation.9 | async-start | bytes 2228224 | tf_op jit(solution)/shard_map/all_gather | solution.py:20
  687.7 69.7 %copy-start = (f32[128,256]{1,0:T(8,128)S(1)}, f32[128,256]{1,0:T(8,128)}, u32[]{:S(2)}) copy-start(f32[128,256]{1,0:T(8,128)} %fusion.30) | copy-start | bytes 393220
  687.7 182.0 %all-reduce.5.cloned.1.call-start = ((), (), s32[]{:S(2)}) async-start(), calls=%async_computation.10 | async-start | bytes 131072 | tf_op jit(solution)/shard_map/psum | solution.py:46
Sparse Core Ops, SparseCore 0:
  11.0 64.3 all-gather.9
  82.5 59.6 all-gather.11
  149.4 59.6 all-gather.13
  216.2 59.6 all-gather.15
  283.1 59.6 all-gather.17
  349.9 59.6 all-gather.19
  416.8 59.6 all-gather.21
  483.6 59.6 all-gather.23
  550.8 111.1 all-reduce.2
  687.8 62.4 all-gather.25
  758.5 111.1 all-reduce.4
where the time goes:
time: 888 us; the launch traced here: 880 us
  waiting for transfers between devices  767 us (86%)
  matrix products  66.2 us (7%)
  other arithmetic  23.7 us (3%)
  between operations  16.8 us (2%)
    all_gather x9, waiting for transfers between devices, apply_factor(): lax.all_gather(vectors, 'blk', axis=0, tiled=True)  544 us
    psum x1, waiting for transfers between devices, local(): lax.psum(lax.dot_general(current, current, (((0,), (0,)), ((), ())), prec...  111 us
    psum x1, waiting for transfers between devices, local(): lax.psum(lax.dot_general(basis_rows, mapped, (((0,), (0,)), ((), ())), pr...  111 us
    dot_general x10, matrix products, local_dot(): jnp.dot(left_side, right_side, precision=lax.Precision.HIGHEST, preferred...  63.3 us
  transfers between devices with their start and end apart: 11, of which 11 were waited for; matrix products, arithmetic and copies ran while one was open for 0% of the time, Pallas kernels for 0%

commit v1 on v0

--- a/solution.py
+++ b/solution.py
@@ -43,7 +43,8 @@
     cholesky_low = jnp.linalg.cholesky(gram_matrix)
     basis_rows = lower_solve(cholesky_low, current.T).T
     mapped = apply_factor(factor, basis_rows)
-    projected = lax.psum(
+    vectors_press = lambda s0, link_axis: lax.all_gather(s0, axis_name=link_axis).sum(axis=0)
+    projected = vectors_press(
         lax.dot_general(
             basis_rows,
             mapped,
@@ -51,7 +52,7 @@
             precision=lax.Precision.HIGHEST,
             preferred_element_type=jnp.float32,
         ),
-        "blk",
+        link_axis="blk",
     )
     residual = mapped - local_dot(basis_rows, projected)
     return (basis_rows, projected, residual)

time: 888 us -> 833 us (0.938)
  the two profiles are of different devices: /device:TPU:2 before, /device:TPU:32 now
where the time goes in v1:
time: 833 us; the launch traced here: 825 us
  waiting for transfers between devices  713 us (86%)
  matrix products  65.4 us (8%)
  other arithmetic  25 us (3%)
  between operations  16.8 us (2%)
    all_gather x9, waiting for transfers between devices, apply_factor(): lax.all_gather(vectors, 'blk', axis=0, tiled=True)  544 us
    psum x1, waiting for transfers between devices, local(): lax.psum(lax.dot_general(current, current, (((0,), (0,)), ((), ())), prec...  111 us
    dot_general x10, matrix products, local_dot(): jnp.dot(left_side, right_side, precision=lax.Precision.HIGHEST, preferred...  62.5 us
    all_gather x1, waiting for transfers between devices, local(): lax.all_gather(s0, axis_name=link_axis).sum(axis=0)  56.9 us
  transfers between devices with their start and end apart: 11, of which 11 were waited for; matrix products, arithmetic and copies ran while one was open for 0% of the time, Pallas kernels for 0%

profile of v1, /device:TPU:32, one launch (start us, length us, event | category | flops | bytes accessed | tf_op | source)
XLA Modules:
  0.0 825.1 jit_solution(13330392497979138388)
XLA Ops:
  7.2 0.0 all-gather.12.cloned.1.call-start
  7.2 0.7 all-gather.12.cloned.1.call-update
  7.9 0.0 all-gather.14.cloned.1.call-start
  7.9 1.3 fusion.33
  11.9 63.5 %all-gather.12.cloned.1.call-done = f32[4096,128]{1,0:T(8,128)} async-done(((f32[256,128]{1,0:T(8,128)}), f32[4096,128]{1,0:T(8,128)}) %all-gather.12.cloned.1.call-update) | async-done | bytes 2097168 | tf_op jit(solution)/shard_map/all_gather | solution.py:20
  75.4 7.0 fusion.28
  82.4 0.0 all-gather.14.cloned.1.call-update
  82.4 0.0 copy-start.6
  82.4 0.0 all-gather.16.cloned.1.call-start
  82.4 59.8 %all-gather.14.cloned.1.call-done = f32[4096,128]{1,0:T(8,128)} async-done(((f32[256,128]{1,0:T(8,128)}), f32[4096,128]{1,0:T(8,128)}) %all-gather.14.cloned.1.call-update) | async-done | bytes 2097168 | tf_op jit(solution)/shard_map/all_gather | solution.py:20
  142.2 7.0 fusion.27
  149.2 0.0 all-gather.16.cloned.1.call-update
  149.2 0.0 copy-start.5
  149.2 0.0 all-gather.18.cloned.1.call-start
  149.3 59.8 %all-gather.16.cloned.1.call-done = f32[4096,128]{1,0:T(8,128)} async-done(((f32[256,128]{1,0:T(8,128)}), f32[4096,128]{1,0:T(8,128)}) %all-gather.16.cloned.1.call-update) | async-done | bytes 2097168 | tf_op jit(solution)/shard_map/all_gather | solution.py:20
  209.1 7.0 fusion.23
  216.0 0.0 all-gather.18.cloned.1.call-update
  216.1 0.0 copy-start.2
  216.1 0.5 all-gather.20.cloned.1.call-start
  216.6 59.3 %all-gather.18.cloned.1.call-done = f32[4096,128]{1,0:T(8,128)} async-done(((f32[256,128]{1,0:T(8,128)}), f32[4096,128]{1,0:T(8,128)}) %all-gather.18.cloned.1.call-update) | async-done | bytes 2097168 | tf_op jit(solution)/shard_map/all_gather | solution.py:20
  275.9 7.0 fusion.19
  282.9 0.0 all-gather.20.cloned.1.call-update
  282.9 0.0 copy-start.3
  282.9 0.0 all-gather.22.cloned.1.call-start
  283.0 59.8 %all-gather.20.cloned.1.call-done = f32[4096,128]{1,0:T(8,128)} async-done(((f32[256,128]{1,0:T(8,128)}), f32[4096,128]{1,0:T(8,128)}) %all-gather.20.cloned.1.call-update) | async-done | bytes 2097168 | tf_op jit(solution)/shard_map/all_gather | solution.py:20
  342.8 7.0 fusion.15
  349.8 0.0 all-gather.22.cloned.1.call-update
  349.8 0.0 copy-start.4
  349.8 0.0 all-gather.24.cloned.1.call-start
  349.8 59.8 %all-gather.22.cloned.1.call-done = f32[4096,128]{1,0:T(8,128)} async-done(((f32[256,128]{1,0:T(8,128)}), f32[4096,128]{1,0:T(8,128)}) %all-gather.22.cloned.1.call-update) | async-done | bytes 2097168 | tf_op jit(solution)/shard_map/all_gather | solution.py:20
  409.6 7.0 fusion.11
  416.6 0.0 all-gather.24.cloned.1.call-update
  416.6 0.0 copy-start.1
  416.6 0.2 all-gather.26.cloned.1.call-start
  416.9 59.6 %all-gather.24.cloned.1.call-done = f32[4096,128]{1,0:T(8,128)} async-done(((f32[256,128]{1,0:T(8,128)}), f32[4096,128]{1,0:T(8,128)}) %all-gather.24.cloned.1.call-update) | async-done | bytes 2097168 | tf_op jit(solution)/shard_map/all_gather | solution.py:20
  476.5 7.0 fusion.7
  483.5 0.0 all-gather.26.cloned.1.call-update
  483.5 0.0 all-reduce.2.cloned.1.call-start
  483.5 59.8 %all-gather.26.cloned.1.call-done = f32[4096,128]{1,0:T(8,128)} async-done(((f32[256,128]{1,0:T(8,128)}), f32[4096,128]{1,0:T(8,128)}) %all-gather.26.cloned.1.call-update) | async-done | bytes 2097168 | tf_op jit(solution)/shard_map/all_gather | solution.py:20
  543.3 6.3 fusion.3
  549.7 1.0 fusion.34
  550.7 0.0 all-reduce.2.cloned.1.call-update
  550.7 0.3 all-gather.28.cloned.1.call-start
  551.0 111.0 %all-reduce.2.cloned.1.call-done = f32[128,128]{0,1:T(8,128)} async-done(((f32[128,128]{0,1:T(8,128)}), f32[128,128]{0,1:T(8,128)}) %all-reduce.2.cloned.1.call-update) | async-done | bytes 65552 | tf_op jit(solution)/shard_map/psum | solution.py:33
  662.0 0.9 copy.14
  662.9 0.9 fusion.32
  663.8 11.7 %cholesky.16 = f32[128,128]{1,0:T(8,128)S(1)} custom-call(f32[128,128]{1,0:T(8,128)S(1)} %fusion.32), custom_call_target="Cholesky" | custom-call | tf_op jit(solution)/shard_map/jit(cholesky)/cholesky | solution.py:43
  675.5 0.6 compare_reduce_fusion
  676.1 0.7 fusion.29
  676.8 9.8 %custom-call.6 = f32[1,128,128]{1,2,0:T(8,128)S(1)} custom-call(f32[1,128,128]{2,1,0:T(8,128)S(1)} %fusion.29), custom_call_target="InvertDiagBlocksLowerTriangular" | custom-call | tf_op jit(solution)/shard_map/triangular_solve | solution.py:16
  686.6 1.0 fusion.30
  687.6 0.0 all-gather.28.cloned.1.call-update
  687.6 0.0 copy-start
  687.6 0.0 all-gather.30.cloned.1.call-start
  687.7 62.5 %all-gather.28.cloned.1.call-done = f32[4096,128]{0,1:T(8,128)} async-done(((f32[256,128]{0,1:T(8,128)}), f32[4096,128]{0,1:T(8,128)}) %all-gather.28.cloned.1.call-update) | async-done | bytes 2097168 | tf_op jit(solution)/shard_map/all_gather | solution.py:20
  750.2 7.1 fusion.35
  757.4 0.9 fusion.36
  758.3 0.0 all-gather.30.cloned.1.call-update
  758.3 0.8 copy.16
  759.0 56.9 %all-gather.30.cloned.1.call-done = f32[2048,128]{1,0:T(8,128)} async-done(((f32[128,128]{1,0:T(8,128)}), f32[2048,128]{1,0:T(8,128)}) %all-gather.30.cloned.1.call-update) | async-done | bytes 1048592 | tf_op jit(solution)/shard_map/all_gather | solution.py:46
  816.0 1.3 reduce_sum.9
  817.2 0.0 copy-start.8
  817.3 0.3 convolution_subtract_fusion.1
  817.6 0.8 copy.17
  (11 shorter events, 0.1 us)
Async XLA Ops:
  7.2 68.2 %all-gather.12.cloned.1.call-start = ((), (), s32[]{:S(2)}) async-start(), calls=%async_computation | async-start | bytes 2228224 | tf_op jit(solution)/shard_map/all_gather | solution.py:20
  7.9 134.3 %all-gather.14.cloned.1.call-start = ((), (), s32[]{:S(2)}) async-start(), calls=%async_computation.1 | async-start | bytes 2228224 | tf_op jit(solution)/shard_map/all_gather | solution.py:20
  75.4 66.9 %copy-start.7 = (f32[256,128]{1,0:T(8,128)S(1)}, f32[256,128]{1,0:T(8,128)}, u32[]{:S(2)}) copy-start(f32[256,128]{1,0:T(8,128)} %param.4) | copy-start | bytes 393220
  82.4 126.7 %copy-start.6 = (f32[256,128]{1,0:T(8,128)S(1)}, f32[256,128]{1,0:T(8,128)}, u32[]{:S(2)}) copy-start(f32[256,128]{1,0:T(8,128)} %fusion.28) | copy-start | bytes 393220
  82.4 126.7 %all-gather.16.cloned.1.call-start = ((), (), s32[]{:S(2)}) async-start(), calls=%async_computation.2 | async-start | bytes 2228224 | tf_op jit(solution)/shard_map/all_gather | solution.py:20
  149.2 126.7 %copy-start.5 = (f32[256,128]{1,0:T(8,128)S(1)}, f32[256,128]{1,0:T(8,128)}, u32[]{:S(2)}) copy-start(f32[256,128]{1,0:T(8,128)} %fusion.27) | copy-start | bytes 393220
  149.2 126.7 %all-gather.18.cloned.1.call-start = ((), (), s32[]{:S(2)}) async-start(), calls=%async_computation.3 | async-start | bytes 2228224 | tf_op jit(solution)/shard_map/all_gather | solution.py:20
  216.1 126.7 %copy-start.2 = (f32[256,128]{1,0:T(8,128)S(1)}, f32[256,128]{1,0:T(8,128)}, u32[]{:S(2)}) copy-start(f32[256,128]{1,0:T(8,128)} %fusion.23) | copy-start | bytes 393220
  216.1 126.7 %all-gather.20.cloned.1.call-start = ((), (), s32[]{:S(2)}) async-start(), calls=%async_computation.4 | async-start | bytes 2228224 | tf_op jit(solution)/shard_map/all_gather | solution.py:20
  282.9 126.7 %copy-start.3 = (f32[256,128]{1,0:T(8,128)S(1)}, f32[256,128]{1,0:T(8,128)}, u32[]{:S(2)}) copy-start(f32[256,128]{1,0:T(8,128)} %fusion.19) | copy-start | bytes 393220
  282.9 126.7 %all-gather.22.cloned.1.call-start = ((), (), s32[]{:S(2)}) async-start(), calls=%async_computation.5 | async-start | bytes 2228224 | tf_op jit(solution)/shard_map/all_gather | solution.py:20
  349.8 126.7 %copy-start.4 = (f32[256,128]{1,0:T(8,128)S(1)}, f32[256,128]{1,0:T(8,128)}, u32[]{:S(2)}) copy-start(f32[256,128]{1,0:T(8,128)} %fusion.15) | copy-start | bytes 393220
  349.8 126.7 %all-gather.24.cloned.1.call-start = ((), (), s32[]{:S(2)}) async-start(), calls=%async_computation.6 | async-start | bytes 2228224 | tf_op jit(solution)/shard_map/all_gather | solution.py:20
  416.6 126.7 %copy-start.1 = (f32[256,128]{1,0:T(8,128)S(1)}, f32[256,128]{1,0:T(8,128)}, u32[]{:S(2)}) copy-start(f32[256,128]{1,0:T(8,128)} %fusion.11) | copy-start | bytes 393220
  416.6 126.7 %all-gather.26.cloned.1.call-start = ((), (), s32[]{:S(2)}) async-start(), calls=%async_computation.7 | async-start | bytes 2228224 | tf_op jit(solution)/shard_map/all_gather | solution.py:20
  483.5 178.5 %all-reduce.2.cloned.1.call-start = ((), (), s32[]{:S(2)}) async-start(), calls=%async_computation.8 | async-start | bytes 131072 | tf_op jit(solution)/shard_map/psum | solution.py:33
  550.7 199.5 %all-gather.28.cloned.1.call-start = ((), (), s32[]{:S(2)}) async-start(), calls=%async_computation.9 | async-start | bytes 2228224 | tf_op jit(solution)/shard_map/all_gather | solution.py:20
  687.6 69.7 %copy-start = (f32[128,256]{1,0:T(8,128)S(1)}, f32[128,256]{1,0:T(8,128)}, u32[]{:S(2)}) copy-start(f32[128,256]{1,0:T(8,128)} %fusion.30) | copy-start | bytes 393220
  687.6 128.3 %all-gather.30.cloned.1.call-start = ((), (), s32[]{:S(2)}) async-start(), calls=%async_computation.10 | async-start | bytes 1114112 | tf_op jit(solution)/shard_map/all_gather | solution.py:46
  817.2 1.1 copy-start.8
Sparse Core Ops, SparseCore 0:
  11.0 64.3 all-gather.11
  82.5 59.6 all-gather.13
  149.3 59.6 all-gather.15
  216.2 59.6 all-gather.17
  283.1 59.6 all-gather.19
  349.9 59.6 all-gather.21
  416.8 59.6 all-gather.23
  483.6 59.6 all-gather.25
  550.8 111.0 all-reduce.1
  687.7 62.4 all-gather.27
  758.4 57.5 all-gather.29
